TPU v7x, 128 devices: a whole 4x4x4 slice. The times are simulated.
128 devices in a mesh: dp: 4 (over z), tensor: 32 (over x, y, core).
Axes of the slice: x: 4, y: 4, z: 4, core: 2. Of those that a mesh axis runs over, the one named last changes fastest.
Arguments:
- tokens: bfloat16 [256, 128, 1536], P(('dp', 'tensor')), may hold values from -60 to 60
- cached: bfloat16 [256, 512, 1536], P(('dp', 'tensor')), may hold values from -60 to 60
- norm_gains: float32 [2, 1536], replicated, may hold values from 0.5 to 1.5
- w_qkv: bfloat16 [1536, 3072], replicated, may hold values from -0.15625 to 0.15625
- w_out: bfloat16 [1536, 1536], replicated, may hold values from -0.15625 to 0.15625
- mlp_weights: bfloat16 [3, 1536, 4096], P(None, None, 'tensor'), may hold values from -0.15625 to 0.15625
- request_order: int32 [256], replicated, may hold values from 0 to 255, as said below
- new_lengths: int32 [256], replicated, may hold values from 1 to 128, 20480 in all
- cached_lengths: int32 [256], replicated, may hold values from 0 to 384
- decode_slots: int32 [256], replicated, may hold values from 0 to 255, as said below
Outputs:
- layer_out: bfloat16 [256, 128, 1536], P(('dp', 'tensor'))
- kv_decode: bfloat16 [256, 512, 1536], P('dp', 'tensor')
Inputs may be any that keep to these rules, and one draw needn't show every extreme that they name: `request_order`: each value once; the device at index k of dp+tensor holds prefill slots k * 2 to (k + 1) * 2 - 1. `decode_slots`: each value once; the 64 requests held by the prefill slots of one index of dp take exactly 16 slots of every aligned block of 64 decode slots.
All inputs are finite; a program needn't handle non-finite values.
Results may differ from a plain program's by a relative error of at most 0.015.
Values may be sent and summed in bfloat16 or wider, within the bound.
A program may use at most 192 MiB of HBM per device.

v0:
```python
import jax
import jax.numpy as jnp
from jax import lax
from jax.sharding import PartitionSpec as P

D = 1536
HEADS = 16
KV_HEADS = 8
HEAD_DIM = 96
NEW = 128
CTX = 512


epsilon = 1e-05
rope_base = 100000.0


def norm_rows(values, gain):
    widened = values.astype(jnp.float32)
    factor = lax.rsqrt(jnp.mean(widened * widened, axis=-1, keepdims=True) + epsilon)
    return (widened * factor * gain).astype(jnp.bfloat16)


def rotate(values, positions):
    half_dim = values.shape[-1] // 2
    frequency = rope_base ** (-2.0 * jnp.arange(half_dim, dtype=jnp.float32) / values.shape[-1])
    angles = positions[:, None, None] * frequency
    cosine = jnp.cos(angles)
    sine_part = jnp.sin(angles)
    leading = values[..., :half_dim]
    trailing = values[..., half_dim:]
    return jnp.concatenate(
        [leading * cosine - trailing * sine_part, trailing * cosine + leading * sine_part], axis=-1
    )


def place_context(fresh_rows, cached_rows, new_count, cached_count):
    offsets = jnp.arange(NEW, dtype=jnp.int32)
    kept = jnp.where((offsets < new_count)[:, None], fresh_rows, jnp.zeros_like(fresh_rows))
    canvas = jnp.zeros((CTX, fresh_rows.shape[1]), fresh_rows.dtype)
    placed = lax.dynamic_update_slice_in_dim(canvas, kept, cached_count, 0)
    spots = jnp.arange(CTX, dtype=jnp.int32)
    return jnp.where((spots < cached_count)[:, None], cached_rows, placed)


def attend(queries, context, cached_count):
    group_size = HEADS // KV_HEADS
    key_width = KV_HEADS * HEAD_DIM
    key_heads = context[:, :key_width].reshape(CTX, KV_HEADS, HEAD_DIM)
    value_heads = context[:, key_width:].reshape(CTX, KV_HEADS, HEAD_DIM)
    grouped = queries.reshape(NEW, KV_HEADS, group_size, HEAD_DIM)
    scores = jnp.einsum(
        "qkgd,pkd->kgqp", grouped, key_heads, preferred_element_type=jnp.float32
    ) * HEAD_DIM ** (-0.5)
    last_key = cached_count + jnp.arange(NEW, dtype=jnp.int32)
    allowed = jnp.arange(CTX, dtype=jnp.int32)[None, :] <= last_key[:, None]
    scores = jnp.where(allowed, scores, -jnp.inf)
    highest = jnp.max(scores, axis=-1, keepdims=True)
    exponent = jnp.exp(scores - highest)
    weights = (exponent / jnp.sum(exponent, axis=-1, keepdims=True)).astype(jnp.bfloat16)
    attended = jnp.einsum(
        "kgqp,pkd->qkgd", weights, value_heads, preferred_element_type=jnp.float32
    )
    return attended.reshape(NEW, D).astype(jnp.bfloat16)


def lookup(source_table, wanted):
    every_index = jnp.arange(source_table.shape[0], dtype=jnp.int32)
    matches = wanted[:, None] == every_index[None, :]
    return jnp.sum(jnp.where(matches, source_table[None, :], 0), axis=1)


def locate(source_table, wanted):
    every_index = jnp.arange(source_table.shape[0], dtype=jnp.int32)
    matches = source_table[None, :] == wanted[:, None]
    return jnp.sum(jnp.where(matches, every_index[None, :], 0), axis=1)


def block_sums(activated, down_part, unit_width):
    blocks = activated.shape[1] // unit_width
    spread = activated.reshape(activated.shape[0], blocks, unit_width)
    down_spread = down_part.reshape(down_part.shape[0], blocks, unit_width)
    partial_sums = jnp.einsum(
        "rmw,dmw->mrd", spread, down_spread, preferred_element_type=jnp.float32
    ).astype(jnp.bfloat16)
    return jnp.sum(partial_sums.astype(jnp.float32), axis=0)


def local(
    tokens,
    cached,
    norm_gains,
    w_qkv,
    w_out,
    mlp_weights,
    request_order,
    new_lengths,
    cached_lengths,
    decode_slots,
):
    tensor_size = lax.axis_size("tensor")
    group_total = lax.axis_size("dp")
    local_reqs = tokens.shape[0]
    group_reqs = local_reqs * tensor_size
    group_index = lax.axis_index("dp")
    device_index = group_index * tensor_size + lax.axis_index("tensor")
    local_order = lax.dynamic_slice_in_dim(request_order, device_index * local_reqs, local_reqs)
    new_counts = lookup(new_lengths, local_order)
    cached_counts = lookup(cached_lengths, local_order)
    key_width = KV_HEADS * HEAD_DIM
    row_count = local_reqs * NEW
    flattened = tokens.reshape(row_count, D)
    normed = norm_rows(flattened, norm_gains[0])
    projected = jnp.dot(normed, w_qkv, preferred_element_type=jnp.float32)
    positions = (
        (cached_counts[:, None] + jnp.arange(NEW, dtype=jnp.int32)[None, :])
        .reshape(row_count)
        .astype(jnp.float32)
    )
    queries = rotate(projected[:, :D].reshape(row_count, HEADS, HEAD_DIM), positions).astype(
        jnp.bfloat16
    )
    key_rows = rotate(
        projected[:, D : D + key_width].reshape(row_count, KV_HEADS, HEAD_DIM), positions
    ).reshape(row_count, key_width)
    fresh_rows = jnp.concatenate([key_rows, projected[:, D + key_width :]], axis=1).astype(
        jnp.bfloat16
    )
    fresh_rows = fresh_rows.reshape(local_reqs, NEW, 2 * key_width)
    contexts = jax.vmap(place_context)(fresh_rows, cached, new_counts, cached_counts)
    attended = lax.map(
        lambda inputs: attend(inputs[0], inputs[1], inputs[2]),
        (queries.reshape(local_reqs, NEW, HEADS, HEAD_DIM), contexts, cached_counts),
    )
    attended = attended.reshape(row_count, D)
    residual = (
        flattened.astype(jnp.float32) + jnp.dot(attended, w_out, preferred_element_type=jnp.float32)
    ).astype(jnp.bfloat16)
    post_norm = norm_rows(residual, norm_gains[1])
    unit_width = mlp_weights.shape[2]
    shards = lax.all_gather(mlp_weights, "tensor", axis=2, tiled=True)
    gate_out = jnp.dot(post_norm, shards[0], preferred_element_type=jnp.float32)
    up_out = jnp.dot(post_norm, shards[1], preferred_element_type=jnp.float32)
    activated = (jax.nn.silu(gate_out) * up_out).astype(jnp.bfloat16)
    mlp_sum = block_sums(activated, shards[2], unit_width)
    live = (jnp.arange(NEW, dtype=jnp.int32)[None, :] < new_counts[:, None]).reshape(row_count, 1)
    layer_out = (
        jnp.where(live, residual.astype(jnp.float32) + mlp_sum, 0.0)
        .astype(jnp.bfloat16)
        .reshape(local_reqs, NEW, D)
    )
    slot_ids = group_index * group_reqs + jnp.arange(group_reqs, dtype=jnp.int32)
    request_at = locate(decode_slots, slot_ids)
    prefill_at = locate(request_order, request_at)
    exchanged = lax.all_to_all(contexts, "tensor", split_axis=1, concat_axis=0, tiled=True)
    group_order = lax.dynamic_slice_in_dim(request_order, group_index * group_reqs, group_reqs)
    row_slots = lookup(decode_slots, group_order)
    arranged = exchanged[jnp.argsort(row_slots)]
    arrived = lax.all_to_all(arranged, "dp", split_axis=0, concat_axis=0, tiled=True)
    per_group = group_reqs // group_total
    owners = prefill_at // group_reqs
    ordinal = jnp.arange(group_reqs, dtype=jnp.int32)
    same_owner = (owners[:, None] == owners[None, :]) & (ordinal[None, :] < ordinal[:, None])
    source_rows = owners * per_group + jnp.sum(same_owner.astype(jnp.int32), axis=1)
    kv_decode = arrived[source_rows]
    return (layer_out, kv_decode)


def solution(mesh):
    in_specs = (
        P(("dp", "tensor"), None, None),
        P(("dp", "tensor"), None, None),
        P(),
        P(),
        P(),
        P(None, None, "tensor"),
        P(),
        P(),
        P(),
        P(),
    )
    out_specs = (P(("dp", "tensor"), None, None), P("dp", "tensor", None))
    return jax.shard_map(local, mesh=mesh, in_specs=in_specs, out_specs=out_specs, check_vma=False)
```

profile of v0, /device:TPU:66, one launch (start us, length us, event | category | flops | bytes accessed | tf_op | source)
XLA Modules:
  0.0 244.7 jit_solution(8965223898285327446)
XLA Ops:
  7.2 2.5 %copy.73 = bf16[3,1536,128]{1,2,0:T(8,128)(2,1)} copy(bf16[3,1536,128]{2,1,0:T(8,128)(2,1)} %param.17) | data formatting | bytes 2359296 | tf_op args[5]
  10.3 5.2 %fusion.28 = f32[256,3072]{1,0:T(8,128)S(1)} fusion(bf16[256,1536]{1,0:T(8,128)(2,1)S(1)} %fusion.21, bf16[1536,3072]{1,0:T(8,128)(2,1)} %param.15), kind=kOutput, calls=%fused_computation.95 | convolution fusion | flops 2415919104 | bytes 13369344 | tf_op jit(solution)/shard_map/dot_general | solution.py:114
  15.6 1.6 copy-done.1
  20.7 7.0 %broadcast_select_fusion.1 = bf16[2,128,1536]{1,0,2:T(2,128)(2,1)S(1)} fusion(pred[2,128]{1,0:T(4,128)(4,1)S(1)} %get-tuple-element.123, bf16[2,128,768]{1,0,2:T(2,128)(2,1)S(1)} %copy.63, bf16[2,128,768]{1,0,2:T(2,128)(2,1)S(1)} %concatenate.27), kind=kLoop, calls=%fused_computation.44 | loop fusion | flops 786432 | bytes 1573120 | tf_op jit(solution)/shard_map/vmap(jit(_where))/select_n | solution.py:39
  27.7 1.8 copy.65
  30.4 21.6 %while.12 = (s32[]{:T(128)}, bf16[2,512,1536]{2,1,0:T(8,128)(2,1)S(1)}, s32[2,3]{1,0:T(2,128)}, bf16[2,128,1536]{2,1,0:T(8,128)(2,1)}, s32[]{:T(128)}, /*index=5*/s32[3]{0:T(128)S(1)}, s32[]{:T(128)}) while((s32[]{:T(128)}, bf16[2,512,1536]{2,1,0:T(8,128)(2,1)S(1)}, s32[2,3]{1,0:T(2,128)}, bf16[2,128,1536]{2,1,0:T(8,128)(2,1)}, s32[]{:T(128)}, ...), condition=%wide.while_cond, body=%wide.while_body.sunk | while | flops 196627 | bytes 1966259 | solution.py:41
  31.8 2.8 %and_reduce_fusion.2 = pred[]{:T(512)} fusion(s32[3]{0:T(128)S(1)} %get-tuple-element.215, s32[1]{0:T(128)} %bitcast.134, s32[1]{0:T(128)} %bitcast.135, s32[1]{0:T(128)} %bitcast.136), kind=kLoop, calls=%fused_computation.21.clone.1 | loop fusion | flops 17 | bytes 25 | tf_op jit(solution)/shard_map/vmap(vmap())/scatter
  34.6 3.2 %dynamic-slice_select_fusion.2 = bf16[1,128,1536]{2,1,0:T(8,128)(2,1)S(1)} fusion(bf16[2,128,1536]{2,1,0:T(8,128)(2,1)} %get-tuple-element.213, s32[]{:T(128)S(6)} %copy.97, bf16[2,512,1536]{2,1,0:T(8,128)(2,1)S(1)} %get-tuple-element.204, s32[]{:T(128)} %bitcast.132, s32[]{:T(128)} %bitcast.133, pred[]{:T(512)} %and_reduce_fusion.2), kind=kLoop, calls=%fused_computation.20.clone.1 | loop fusion | flops 196608 | bytes 1179661 | tf_op jit(solution)/shard_map/vmap(vmap())/scatter
  37.8 3.4 %dynamic-update-slice.3 = bf16[2,512,1536]{2,1,0:T(8,128)(2,1)S(1)} dynamic-update-slice(bf16[2,512,1536]{2,1,0:T(8,128)(2,1)S(1)} %get-tuple-element.204, bf16[1,128,1536]{2,1,0:T(8,128)(2,1)S(1)} %dynamic-slice_select_fusion.2, s32[]{:T(128)} %bitcast.132, s32[]{:T(128)} %bitcast.133, s32[]{:T(128)} %constant.39.clone.1..sunk) | dynamic-update-slice | bytes 786436 | tf_op jit(solution)/shard_map/vmap(vmap())/scatter
  42.6 2.8 %and_reduce_fusion.2 = pred[]{:T(512)} fusion(s32[3]{0:T(128)S(1)} %get-tuple-element.215, s32[1]{0:T(128)} %bitcast.134, s32[1]{0:T(128)} %bitcast.135, s32[1]{0:T(128)} %bitcast.136), kind=kLoop, calls=%fused_computation.21.clone.1 | loop fusion | flops 17 | bytes 25 | tf_op jit(solution)/shard_map/vmap(vmap())/scatter
  45.4 3.2 %dynamic-slice_select_fusion.2 = bf16[1,128,1536]{2,1,0:T(8,128)(2,1)S(1)} fusion(bf16[2,128,1536]{2,1,0:T(8,128)(2,1)} %get-tuple-element.213, s32[]{:T(128)S(6)} %copy.97, bf16[2,512,1536]{2,1,0:T(8,128)(2,1)S(1)} %get-tuple-element.204, s32[]{:T(128)} %bitcast.132, s32[]{:T(128)} %bitcast.133, pred[]{:T(512)} %and_reduce_fusion.2), kind=kLoop, calls=%fused_computation.20.clone.1 | loop fusion | flops 196608 | bytes 1179661 | tf_op jit(solution)/shard_map/vmap(vmap())/scatter
  48.6 3.4 %dynamic-update-slice.3 = bf16[2,512,1536]{2,1,0:T(8,128)(2,1)S(1)} dynamic-update-slice(bf16[2,512,1536]{2,1,0:T(8,128)(2,1)S(1)} %get-tuple-element.204, bf16[1,128,1536]{2,1,0:T(8,128)(2,1)S(1)} %dynamic-slice_select_fusion.2, s32[]{:T(128)} %bitcast.132, s32[]{:T(128)} %bitcast.133, s32[]{:T(128)} %constant.39.clone.1..sunk) | dynamic-update-slice | bytes 786436 | tf_op jit(solution)/shard_map/vmap(vmap())/scatter
  52.0 16.8 %broadcast_select_fusion = bf16[2,512,1536]{2,0,1:T(2,128)(2,1)} fusion(pred[2,512]{0,1:T(8,128)(4,1)} %iota_compare_fusion.1, bf16[2,512,1536]{2,1,0:T(8,128)(2,1)S(1)} %get-tuple-element.37, bf16[2,512,1536]{2,1,0:T(8,128)(2,1)} %param.13), kind=kLoop, calls=%fused_computation.28 | loop fusion | flops 1572864 | bytes 9438208 | tf_op jit(solution)/shard_map/vmap(jit(_where))/select_n | solution.py:43
  68.8 8.0 %all-to-all-start = ((bf16[2,512,1536]{2,0,1:T(2,128)(2,1)}), bf16[2,512,1536]{2,0,1:T(2,128)(2,1)}, u32[]{:S(2)}, u32[]{:S(2)}) async-start(bf16[2,512,1536]{2,0,1:T(2,128)(2,1)} %broadcast_select_fusion), calls=%async_computation | async-start | bytes 6291456 | tf_op jit(solution)/shard_map/all_to_all | solution.py:155
  76.8 1.3 slice.82
  78.1 7.0 %copy.70 = bf16[2,512,1536]{1,2,0:T(8,128)(2,1)S(1)} copy(bf16[2,512,1536]{2,0,1:T(2,128)(2,1)} %broadcast_select_fusion) | data formatting | bytes 6291456 | tf_op jit(solution)/shard_map/while | solution.py:131
  85.8 3.0 %copy.68 = f32[256,1536]{0,1:T(8,128)} copy(f32[256,1536]{1,0:T(8,128)} %slice.82) | data formatting | bytes 3145728 | tf_op jit(solution)/shard_map/slice | solution.py:120
  88.8 2.3 subtract_convert_fusion
  91.2 1.8 concatenate.30
  93.0 0.9 concatenate.31
  93.9 2.2 pad_maximum_fusion
  96.1 1.0 copy.71
  97.1 0.9 select_reduce_fusion.1
  98.0 2.1 sort.17
  100.1 47.8 %all-to-all-done = bf16[2,512,1536]{2,0,1:T(2,128)(2,1)} async-done(((bf16[2,512,1536]{2,0,1:T(2,128)(2,1)}), bf16[2,512,1536]{2,0,1:T(2,128)(2,1)}, u32[]{:S(2)}, u32[]{:S(2)}) %all-to-all-start) | async-done | bytes 3145760 | tf_op jit(solution)/shard_map/all_to_all | solution.py:155
  147.8 2.4 copy.76
  150.3 1.9 copy.77
  152.2 4.4 %gather_fusion = bf16[64,16,1536]{2,1,0:T(8,128)(2,1)} fusion(bf16[64,16,1536]{2,1,0:T(8,128)(2,1)} %bitcast.140, s32[1024]{0:T(1024)S(1)} %pad_clamp_fusion.1), kind=kCustom, calls=%fused_computation | custom fusion | bytes 6291712 | tf_op jit(solution)/shard_map/gather | solution.py:158
  156.6 5.3 %all-to-all-start.1 = ((bf16[64,16,1536]{2,1,0:T(8,128)(2,1)}), bf16[64,16,1536]{2,1,0:T(8,128)(2,1)}, u32[]{:S(2)}, u32[]{:S(2)}) async-start(bf16[64,16,1536]{2,1,0:T(8,128)(2,1)} %gather_fusion), calls=%async_computation.1 | async-start | bytes 6291456 | tf_op jit(solution)/shard_map/all_to_all | solution.py:159
  161.9 30.0 %while.11 = (s32[]{:T(128)}, bf16[2,128,1536]{2,1,0:T(8,128)(2,1)}, bf16[2,512,1536]{1,2,0:T(8,128)(2,1)S(1)}, s32[2]{0:T(128)S(1)}, bf16[2,128,16,96]{1,3,2,0:T(8,128)(2,1)}, /*index=5*/s32[]{:T(128)}) while((s32[]{:T(128)}, bf16[2,128,1536]{2,1,0:T(8,128)(2,1)}, bf16[2,512,1536]{1,2,0:T(8,128)(2,1)S(1)}, s32[2]{0:T(128)S(1)}, ...), condition=%wide.region_7.8_spmd, body=%wide.region_4.7_spmd.sunk | while | flops 409207424 | bytes 19547240 | solution.py:131
  163.8 1.0 constant_dynamic-slice_fusion.4
  164.9 1.2 fusion.49
  166.2 5.1 %fusion.50 = (f32[8,2,128]{2,1,0:T(2,128)}, f32[8,2,128,512]{2,3,1,0:T(8,128)}) fusion(pred[128,512]{0,1:T(8,128)(4,1)} %iota_compare_fusion.7, bf16[512,8,96,1]{0,2,3,1:T(8,128)(2,1)} %bitcast.138, bf16[128,8,2,96]{0,3,2,1:T(8,128)(2,1)S(1)} %bitcast.143), kind=kOutput, calls=%fused_computation.93.clone.1 | convolution fusion | flops 205521408 | bytes 5447680 | tf_op jit(solution)/shard_map/while/body/eval_jaxpr/sub | solution.py:59
  171.3 3.6 %fusion.51 = bf16[8,96,2,128]{3,1,2,0:T(8,128)(2,1)} fusion(bf16[512,8,96,1]{0,2,3,1:T(8,128)(2,1)} %bitcast.137, f32[8,2,128,512]{2,3,1,0:T(8,128)} %get-tuple-element.187, f32[8,2,128]{2,1,0:T(2,128)} %get-tuple-element.188), kind=kOutput, calls=%fused_computation.12.clone.1 | convolution fusion | flops 203620352 | bytes 5382144 | tf_op jit(solution)/shard_map/while/body/eval_jaxpr/kgqp,pkd->qkgd/dot_general | solution.py:61
  174.9 1.2 copy.92
  178.8 1.0 constant_dynamic-slice_fusion.4
  179.9 1.2 fusion.49
  181.2 5.1 %fusion.50 = (f32[8,2,128]{2,1,0:T(2,128)}, f32[8,2,128,512]{2,3,1,0:T(8,128)}) fusion(pred[128,512]{0,1:T(8,128)(4,1)} %iota_compare_fusion.7, bf16[512,8,96,1]{0,2,3,1:T(8,128)(2,1)} %bitcast.138, bf16[128,8,2,96]{0,3,2,1:T(8,128)(2,1)S(1)} %bitcast.143), kind=kOutput, calls=%fused_computation.93.clone.1 | convolution fusion | flops 205521408 | bytes 5447680 | tf_op jit(solution)/shard_map/while/body/eval_jaxpr/sub | solution.py:59
  186.3 3.6 %fusion.51 = bf16[8,96,2,128]{3,1,2,0:T(8,128)(2,1)} fusion(bf16[512,8,96,1]{0,2,3,1:T(8,128)(2,1)} %bitcast.137, f32[8,2,128,512]{2,3,1,0:T(8,128)} %get-tuple-element.187, f32[8,2,128]{2,1,0:T(2,128)} %get-tuple-element.188), kind=kOutput, calls=%fused_computation.12.clone.1 | convolution fusion | flops 203620352 | bytes 5382144 | tf_op jit(solution)/shard_map/while/body/eval_jaxpr/kgqp,pkd->qkgd/dot_general | solution.py:61
  189.9 1.2 copy.92
  191.8 0.9 select_reduce_fusion
  192.9 4.3 %multiply_reduce_fusion = (f32[256]{0:T(256)S(1)}, f32[256,1536]{1,0:T(8,128)S(1)}) fusion(bf16[256,1536]{1,0:T(8,128)(2,1)} %bitcast.149, bf16[1536,1536]{1,0:T(8,128)(2,1)} %param.16, bf16[256,1536]{1,0:T(8,128)(2,1)} %bitcast.146), kind=kOutput, calls=%fused_computation.42 | convolution fusion | flops 1210318592 | bytes 7865344 | tf_op jit(solution)/shard_map/dot_general | solution.py:137
  197.2 4.3 %gather_fusion.1 = bf16[64,16,1536]{2,1,0:T(8,128)(2,1)} fusion(bf16[64,16,1536]{2,1,0:T(8,128)(2,1)} %all-to-all-done.1, s32[1024]{0:T(1024)S(1)} %pad_clamp_fusion), kind=kCustom, calls=%fused_computation.1 | custom fusion | bytes 6291712 | tf_op jit(solution)/shard_map/gather | solution.py:165
  201.5 10.5 %slice.87 = bf16[1,1536,4096]{1,2,0:T(8,128)(2,1)} slice(bf16[3,1536,4096]{1,2,0:T(8,128)(2,1)} %all-gather.2.cloned.1.call-done), slice={[2:3], [0:1536], [0:4096]} | slice | bytes 25165824 | tf_op jit(solution)/shard_map/slice | solution.py:145
  212.0 6.5 %fusion.12 = f32[256,4096]{1,0:T(8,128)S(1)} fusion(bf16[3,1536,4096]{1,2,0:T(8,128)(2,1)} %all-gather.2.cloned.1.call-done, f32[256,1536]{1,0:T(8,128)S(1)} %get-tuple-element.125, f32[1536]{0:T(1024)S(1)} %get-tuple-element.85, f32[256]{0:T(256)S(1)} %add_rsqrt_fusion), kind=kOutput, calls=%fused_computation.27 | convolution fusion | flops 3222405120 | bytes 18357248 | tf_op jit(solution)/shard_map/dot_general | solution.py:142
  218.5 6.8 %fusion.19 = bf16[32,32,8,128]{3,2,1,0:T(8,128)(2,1)S(1)} fusion(bf16[3,1536,4096]{1,2,0:T(8,128)(2,1)} %all-gather.2.cloned.1.call-done, f32[256,4096]{1,0:T(8,128)S(1)} %fusion.12, f32[256,1536]{1,0:T(8,128)S(1)} %get-tuple-element.125, f32[1536]{0:T(1024)S(1)} %get-tuple-element.85, f32[256]{0:T(256)S(1)} %add_rsqrt_fusion), kind=kOutput, calls=%fused_computation.36 | convolution fusion | flops 3228696576 | bytes 20454400 | tf_op jit(solution)/shard_map/dot_general | solution.py:143
  225.3 11.5 %convert_reduce_fusion = f32[256,1536]{1,0:T(8,128)S(1)} fusion(bf16[1536,32,128]{0,2,1:T(8,128)(2,1)} %bitcast.139, bf16[32,32,8,128]{3,2,1,0:T(8,128)(2,1)S(1)} %fusion.19), kind=kOutput, calls=%fused_computation.23 | convolution fusion | flops 3258580992 | bytes 16252928 | tf_op jit(solution)/shard_map/rmw,dmw->mrd/dot_general | solution.py:83
  236.8 1.1 select_convert_fusion
  (78 shorter events, 14.1 us)
Async XLA Ops:
  7.2 2.6 %copy-start.6 = (f32[2,1536]{1,0:T(2,128)S(1)}, f32[2,1536]{1,0:T(2,128)}, u32[]{:S(2)}) copy-start(f32[2,1536]{1,0:T(2,128)} %param.14) | copy-start | bytes 36868
  7.2 2.6 %copy-start = (bf16[2,128,1536]{2,1,0:T(8,128)(2,1)S(1)}, bf16[2,128,1536]{2,1,0:T(8,128)(2,1)}, u32[]{:S(2)}) copy-start(bf16[2,128,1536]{2,1,0:T(8,128)(2,1)} %param.12) | copy-start | bytes 2359300
  7.2 194.3 %all-gather.2.cloned.1.call-start = ((), (), s32[]{:S(2)}) async-start(), calls=%async_computation.2 | async-start | bytes 38928384 | tf_op jit(solution)/shard_map/all_gather | solution.py:141
  10.3 6.9 %copy-start.9 = (s32[256]{0:T(256)S(1)}, s32[256]{0:T(256)}, u32[]{:S(2)}) copy-start(s32[256]{0:T(256)} %param.18) | copy-start | bytes 3076
  10.3 7.0 %copy-start.7 = (s32[256]{0:T(256)S(1)}, s32[256]{0:T(256)}, u32[]{:S(2)}) copy-start(s32[256]{0:T(256)} %param.19) | copy-start | bytes 3076
  10.3 7.0 %copy-start.8 = (s32[256]{0:T(256)S(1)}, s32[256]{0:T(256)}, u32[]{:S(2)}) copy-start(s32[256]{0:T(256)} %param.20) | copy-start | bytes 3076
  10.3 7.2 %copy-start.12 = (s32[2]{0:T(128)S(1)}, s32[2]{0:T(128)}, u32[]{:S(2)}) copy-start(s32[2]{0:T(128)} %constant.75.clone.1) | copy-start | bytes 28
  15.5 1.6 copy-start.1
  19.3 0.6 copy-start.3
  19.3 0.6 copy-start.4
  20.7 9.7 %copy-start.5 = (s32[3]{0:T(128)S(1)}, s32[3]{0:T(128)}, u32[]{:S(2)}) copy-start(s32[3]{0:T(128)} %constant.169) | copy-start | bytes 40
  68.8 8.0 %copy-start.2 = (f32[256,3072]{1,0:T(8,128)S(1)}, f32[256,3072]{1,0:T(8,128)}, u32[]{:S(2)}) copy-start(f32[256,3072]{1,0:T(8,128)} %copy-done.1) | copy-start | bytes 9437188
  68.8 79.0 %all-to-all-start = ((bf16[2,512,1536]{2,0,1:T(2,128)(2,1)}), bf16[2,512,1536]{2,0,1:T(2,128)(2,1)}, u32[]{:S(2)}, u32[]{:S(2)}) async-start(bf16[2,512,1536]{2,0,1:T(2,128)(2,1)} %broadcast_select_fusion), calls=%async_computation | async-start | bytes 6291456 | tf_op jit(solution)/shard_map/all_to_all | solution.py:155
  78.1 7.0 %copy-start.10 = (s32[256]{0:T(256)S(1)}, s32[256]{0:T(256)}, u32[]{:S(2)}) copy-start(s32[256]{0:T(256)} %param.18) | copy-start | bytes 3076
  156.6 40.6 %all-to-all-start.1 = ((bf16[64,16,1536]{2,1,0:T(8,128)(2,1)}), bf16[64,16,1536]{2,1,0:T(8,128)(2,1)}, u32[]{:S(2)}, u32[]{:S(2)}) async-start(bf16[64,16,1536]{2,1,0:T(8,128)(2,1)} %gather_fusion), calls=%async_computation.1 | async-start | bytes 6291456 | tf_op jit(solution)/shard_map/all_to_all | solution.py:159
  225.3 11.5 %copy-start.11 = (pred[256]{0:T(512)(128)(4,1)S(1)}, pred[256]{0:T(512)(128)(4,1)}, u32[]{:S(2)}) copy-start(pred[256]{0:T(512)(128)(4,1)} %get-tuple-element.122) | copy-start | bytes 772
Sparse Core Ops, SparseCore 0:
  10.3 159.7 all-gather.1
where the time goes:
time: 250 us; the launch traced here: 245 us
  local copies, waits for them, and re-layouts  66.9 us (27%)
  matrix products  51.7 us (21%)
  other arithmetic  50.5 us (20%)
  waiting for transfers between devices  47.8 us (19%)
  between operations  14.4 us (6%)
  starting transfers between devices  13.3 us (5%)
    all_to_all x1, waiting for transfers between devices, local(): lax.all_to_all(contexts, 'tensor', split_axis=1, concat_axis=0, tiled=True)  47.8 us
    select_n x1, other arithmetic, place_context(): return jnp.where((spots < cached_count)[:, None], cached_rows, placed)  16.8 us
    scatter x4, other arithmetic  12 us
    dot_general x1, matrix products, block_sums(): jnp.einsum('rmw,dmw->mrd', spread, down_spread, preferred_element_type=jn...  11.5 us
    slice x1, local copies, waits for them, and re-layouts, local(): mlp_sum = block_sums(activated, shards[2], unit_width)  10.5 us
    sub x2, matrix products, attend(): exponent = jnp.exp(scores - highest)  10.2 us
    scatter x6, local copies, waits for them, and re-layouts  9.58 us
    while x2, local copies, waits for them, and re-layouts, local(): lax.map(lambda inputs: attend(inputs[0], inputs[1], inputs[2]), (queries....  8.07 us
  transfers between devices with their start and end apart: 3, of which 1 were waited for; matrix products, arithmetic and copies ran while one was open for 52% of the time, Pallas kernels for 0%

commit v1 on v0

v1 whole, which is shorter than its diff:
```python
import functools

import jax
import jax.numpy as jnp
import numpy as np
from jax import lax
from jax.experimental import pallas as pl
from jax.experimental.pallas import tpu as pltpu
from jax.sharding import PartitionSpec as P

D = 1536
HEADS = 16
KV_HEADS = 8
HEAD_DIM = 96
NEW = 128
CTX = 512
KEYS = KV_HEADS * HEAD_DIM
RING = 4
CHIPS = RING * RING
MESH = pl.DeviceIdType.MESH

epsilon = 1e-05
rope_base = 100000.0
LANES = 384
TILE = 256
TILES = D // TILE


def messages():
    found = []

    def along(axis, shards, first):
        step = (1, 0) if axis == 0 else (0, 1)
        for shard in shards:
            for sign in (1, -1):
                found.append((shard, first, 2, (sign * step[0], sign * step[1]), "send"))
            for sign in (1, -1):
                source = (shard[0] - sign * step[0], shard[1] - sign * step[1])
                piece = first if sign == 1 else first + 1
                found.append((source, piece, 1, (sign * step[0], sign * step[1]), "pass"))

    along(0, [(0, 0)], 0)
    along(1, [(0, 0)], 2)
    along(1, [(0, 0)], 0)
    along(0, [(0, 0)], 2)
    along(1, [(-1, 0), (1, 0)], 0)
    along(0, [(0, -1), (0, 1)], 2)
    along(1, [(2, 0)], 0)
    along(0, [(0, 2)], 2)
    return found


MESSAGES = messages()
N_MSG = len(MESSAGES)


def wrapped(offset):
    return (offset[0] % RING, offset[1] % RING)


def arrival(message):
    shard, first, count, direction, _ = message
    return wrapped((shard[0] - direction[0], shard[1] - direction[1])), first, count


def stage_of(index):
    shard, first, count, _, _ = MESSAGES[index]
    if wrapped(shard) == (0, 0):
        return 0
    return 1 + max(stage_of(other) for other in sources(index))


def sources(index):
    shard, first, count, _, _ = MESSAGES[index]
    found = []
    for piece in range(first, first + count):
        for other, message in enumerate(MESSAGES):
            came, start, number = arrival(message)
            if came == wrapped(shard) and start <= piece < start + number:
                found.append(other)
    return sorted(set(found))


def norm_rows(values, gain):
    widened = values.astype(jnp.float32)
    factor = lax.rsqrt(jnp.mean(widened * widened, axis=-1, keepdims=True) + epsilon)
    return (widened * factor * gain).astype(jnp.bfloat16)


def dot(a, b):
    return lax.dot_general(a, b, (((1,), (0,)), ((), ())), preferred_element_type=jnp.float32)


def dot_nt(a, b):
    return lax.dot_general(a, b, (((1,), (1,)), ((), ())), preferred_element_type=jnp.float32)


def layer_kernel(
    index_ref,
    tokens_hbm,
    cached_hbm,
    gains_ref,
    turn_ref,
    rope_ref,
    w_qkv_hbm,
    w_out_hbm,
    own_hbm,
    layer_hbm,
    arrived_hbm,
    tokens,
    normed,
    w_qkv,
    w_out,
    context,
    weights,
    queries,
    fresh,
    attended,
    residual,
    posts,
    received_keys,
    received_values,
    arranged,
    activated,
    kept,
    own_sum,
    to_partner,
    from_partner,
    to_pair,
    from_pair,
    local_sem,
    weight_send,
    weight_recv,
    kv_send,
    kv_recv,
    deal_send,
    deal_recv,
    post_send,
    post_recv,
    part_send,
    part_recv,
):
    z = lax.axis_index("dp")
    t = lax.axis_index("tensor")
    x, y, core = t // 8, lax.rem(t // 2, RING), lax.rem(t, 2)
    half = lax.rem(z, 2)
    pair_z = z + 1 - 2 * half
    partner = t + 1 - 2 * core
    member = half * 2 + core

    def tensor_at(dx, dy, other=0):
        there = lax.rem(core + other, 2)
        return (lax.rem(x + dx + RING, RING) * RING + lax.rem(y + dy + RING, RING)) * 2 + there

    def shard_at(offset):
        return lax.rem(x + offset[0] + RING, RING) * RING + lax.rem(y + offset[1] + RING, RING)

    loads = [
        pltpu.make_async_copy(
            own_hbm.at[:, pl.ds(half * 64, 64), :],
            weights.at[:, pl.ds(shard_at((0, 0)) * 64, 64), :],
            local_sem.at[0],
        ),
        pltpu.make_async_copy(tokens_hbm, tokens, local_sem.at[1]),
        pltpu.make_async_copy(w_qkv_hbm, w_qkv, local_sem.at[2]),
        pltpu.make_async_copy(cached_hbm, context, local_sem.at[3]),
        pltpu.make_async_copy(w_out_hbm, w_out, local_sem.at[4]),
    ]
    for load in loads:
        load.start()

    barrier = pltpu.get_barrier_semaphore()

    @pl.loop(1, 32)
    def _(step):
        pl.semaphore_signal(
            barrier, inc=1, device_id=(z, lax.rem(t + step, 32)), device_id_type=MESH
        )

    @pl.loop(1, 4)
    def _(step):
        pl.semaphore_signal(
            barrier, inc=1, device_id=(lax.rem(z + step, 4), t), device_id_type=MESH
        )

    pl.semaphore_wait(barrier, 34)

    def weight_copy(index):
        shard, first, count, direction, _ = MESSAGES[index]
        rows = pl.ds(pl.multiple_of(shard_at(wrapped(shard)) * 64 + 16 * first, 16), 16 * count)
        return pltpu.make_async_remote_copy(
            src_ref=weights.at[:, rows, :],
            dst_ref=weights.at[:, rows, :],
            send_sem=weight_send.at[index],
            recv_sem=weight_recv.at[index],
            device_id=(z, tensor_at(*direction)),
            device_id_type=MESH,
        )

    def weight_arrival(index):
        shard, first, count = arrival(MESSAGES[index])
        rows = pl.ds(pl.multiple_of(shard_at(shard) * 64 + 16 * first, 16), 16 * count)
        pltpu.make_async_remote_copy(
            src_ref=weights.at[:, rows, :],
            dst_ref=weights.at[:, rows, :],
            send_sem=weight_send.at[index],
            recv_sem=weight_recv.at[index],
            device_id=(z, partner),
            device_id_type=MESH,
        ).wait_recv()

    heard = set()

    def weight_stage(number):
        for index in range(N_MSG):
            if stage_of(index) == number:
                for other in sources(index) if number else []:
                    if other not in heard:
                        heard.add(other)
                        weight_arrival(other)
                weight_copy(index).start()

    def weight_rest():
        for index in range(N_MSG):
            if index not in heard:
                weight_arrival(index)
        for index in range(N_MSG):
            weight_copy(index).wait_send()

    loads[0].wait()
    weight_stage(0)

    loads[1].wait()
    for j in range(2):
        normed[pl.ds(j * NEW, NEW), :] = norm_rows(tokens[j], gains_ref[0:1, :])
    loads[2].wait()

    lane = lax.broadcasted_iota(jnp.int32, (NEW, LANES), 1)
    leading = lax.rem(lane, HEAD_DIM) < HEAD_DIM // 2

    def rotated(values, j):
        cosine = turn_ref[j, 0:1, :] * rope_ref[0] - turn_ref[j, 1:2, :] * rope_ref[1]
        sine = turn_ref[j, 2:3, :] * rope_ref[0] + turn_ref[j, 3:4, :] * rope_ref[1]
        parts = []
        for n in range(values.shape[1] // LANES):
            part = values[:, n * LANES : (n + 1) * LANES]
            swapped = jnp.where(
                leading,
                pltpu.roll(part, LANES - HEAD_DIM // 2, 1),
                pltpu.roll(part, HEAD_DIM // 2, 1),
            )
            parts.append((part * cosine + swapped * sine).astype(jnp.bfloat16))
        return jnp.concatenate(parts, axis=1)

    def project(first):
        return dot(normed[...], w_qkv[:, first : first + KEYS])

    keys = project(D)
    for j in range(2):
        fresh[j, :, 0:KEYS] = rotated(keys[j * NEW : (j + 1) * NEW], j)
    values = project(D + KEYS)
    for j in range(2):
        fresh[j, :, KEYS:] = values[j * NEW : (j + 1) * NEW].astype(jnp.bfloat16)

    loads[3].wait()

    @pl.loop(0, 8)
    def _(step):
        j, block = step // 4, lax.rem(step, 4)
        new_count, cached_count = index_ref[64 + j], index_ref[66 + j]
        spot = block * 128 + lax.broadcasted_iota(jnp.int32, (128, NEW), 0)
        order = lax.broadcasted_iota(jnp.int32, (128, NEW), 1)
        chosen = (spot - cached_count == order) & (order < new_count)
        placed = dot(chosen.astype(jnp.bfloat16), fresh[j]).astype(jnp.bfloat16)
        rows = pl.ds(pl.multiple_of(block * 128, 128), 128)
        row = block * 128 + lax.broadcasted_iota(jnp.int32, (128, D), 0)
        context[j, rows, :] = jnp.where(row < cached_count, context[j, rows, :], placed)

    received = (received_keys, received_values)

    def kv_copy(part, step):
        dx, dy, dc = step // 8, lax.rem(step // 2, RING), lax.rem(step, 2)
        target = tensor_at(dx, dy, dc)
        columns = pl.ds(part * KEYS, KEYS)
        return pltpu.make_async_remote_copy(
            src_ref=context.at[:, pl.ds(pl.multiple_of(target * 16, 16), 16), columns],
            dst_ref=received[part].at[t],
            send_sem=kv_send.at[part, step],
            recv_sem=kv_recv.at[part, step],
            device_id=(z, target),
            device_id_type=MESH,
        )

    for part in range(2):

        @pl.loop(1, 32)
        def _(step):
            kv_copy(part, step).start()

    for part in range(2):
        for j in range(2):
            received[part][t, j] = context[
                j, pl.ds(pl.multiple_of(t * 16, 16), 16), part * KEYS : (part + 1) * KEYS
            ]

    for n in range(2):
        some = project(n * KEYS)
        for j in range(2):
            queries[j, :, n * KEYS : (n + 1) * KEYS] = rotated(some[j * NEW : (j + 1) * NEW], j)

    weight_stage(1)

    def attend(j):
        cached_count = index_ref[66 + j]
        spot = lax.broadcasted_iota(jnp.int32, (2 * NEW, CTX), 1)
        order = lax.rem(lax.broadcasted_iota(jnp.int32, (2 * NEW, CTX), 0), NEW)
        allowed = spot <= cached_count + order
        for h in range(KV_HEADS):
            at = h * 2 * HEAD_DIM
            both = jnp.concatenate(
                [queries[j, :, at : at + HEAD_DIM], queries[j, :, at + HEAD_DIM : at + 2 * HEAD_DIM]],
                axis=0,
            )
            key = context[j, :, h * HEAD_DIM : (h + 1) * HEAD_DIM]
            value = context[j, :, KEYS + h * HEAD_DIM : KEYS + (h + 1) * HEAD_DIM]
            scores = dot_nt(both, key) * HEAD_DIM ** (-0.5)
            scores = jnp.where(allowed, scores, -jnp.inf)
            exponent = jnp.exp(scores - jnp.max(scores, axis=-1, keepdims=True))
            total = jnp.sum(exponent, axis=-1, keepdims=True)
            mixed = (dot(exponent.astype(jnp.bfloat16), value) / total).astype(jnp.bfloat16)
            attended[j, :, at : at + 2 * HEAD_DIM] = jnp.concatenate(
                [mixed[:NEW], mixed[NEW:]], axis=1
            )

    def post_copy(kind, j):
        whose = member if kind < 2 else (1 - half) * 2 + core
        rows = posts.at[whose, pl.ds(j * NEW, NEW), :]
        return pltpu.make_async_remote_copy(
            src_ref=rows,
            dst_ref=rows,
            send_sem=post_send.at[kind, j],
            recv_sem=post_recv.at[kind, j],
            device_id=(pair_z, t) if kind == 1 else (z, partner),
            device_id_type=MESH,
        )

    def post_arrival(kind, j):
        whose = (half * 2 + 1 - core, (1 - half) * 2 + core, (1 - half) * 2 + 1 - core)[kind]
        rows = posts.at[whose, pl.ds(j * NEW, NEW), :]
        pltpu.make_async_remote_copy(
            src_ref=rows,
            dst_ref=rows,
            send_sem=post_send.at[kind, j],
            recv_sem=post_recv.at[kind, j],
            device_id=(z, partner),
            device_id_type=MESH,
        ).wait_recv()

    for j in range(2):
        attend(j)
        if j == 0:
            loads[4].wait()
        mixed = dot(attended[j], w_out[...])
        rounded = (tokens[j].astype(jnp.float32) + mixed).astype(jnp.bfloat16)
        residual[j] = rounded
        posts[member, pl.ds(j * NEW, NEW), :] = norm_rows(rounded, gains_ref[1:2, :])
        post_copy(1, j).start()
        post_copy(0, j).start()
        if j == 0:
            weight_stage(2)

    weight_stage(3)

    def deal_copy(part, step):
        target = lax.rem(z + step, 4)
        return pltpu.make_async_remote_copy(
            src_ref=arranged.at[part, pl.ds(pl.multiple_of(target * 16, 16), 16)],
            dst_ref=arrived_hbm.at[part, z],
            send_sem=deal_send.at[part, step],
            recv_sem=deal_recv.at[part, step],
            device_id=(target, t),
            device_id_type=MESH,
        )

    def own_deal(part):
        return pltpu.make_async_copy(
            arranged.at[part, pl.ds(pl.multiple_of(z * 16, 16), 16)],
            arrived_hbm.at[part, z],
            deal_send.at[part, 0],
        )

    def deal(part):
        @pl.loop(1, 32)
        def _(step):
            dx, dy, dc = step // 8, lax.rem(step // 2, RING), lax.rem(step, 2)
            source = (
                lax.rem(x - dx + RING, RING) * RING + lax.rem(y - dy + RING, RING)
            ) * 2 + lax.rem(core + dc, 2)
            pltpu.make_async_remote_copy(
                src_ref=received[part].at[source],
                dst_ref=received[part].at[source],
                send_sem=kv_send.at[part, step],
                recv_sem=kv_recv.at[part, step],
                device_id=(z, partner),
                device_id_type=MESH,
            ).wait_recv()

        @pl.loop(0, 64)
        def _(row):
            slot = index_ref[row]
            arranged[part, row] = received[part][slot // 2, lax.rem(slot, 2)]

        for step in range(1, 4):
            deal_copy(part, step).start()
        own_deal(part).start()

    for j in range(2):
        post_arrival(1, j)
        post_copy(2, j).start()

    deal(0)
    deal(1)

    for j in range(2):
        post_arrival(0, j)
        post_arrival(2, j)
    weight_rest()

    def hidden(which):
        @pl.loop(0, 4)
        def _(step):
            units = pl.ds(pl.multiple_of(step * TILE, TILE), TILE)
            for m in range(2):
                rows = posts[which * 2 + m]
                gate = dot_nt(rows, weights[0, units, :])
                up = dot_nt(rows, weights[1, units, :])
                activated[m, :, units] = (gate / (1.0 + jnp.exp(-gate)) * up).astype(jnp.bfloat16)

    def part_copy(kind, n):
        here, there = ((to_partner.at[0, n], from_partner.at[0, n]), (to_pair.at[n], from_pair.at[n]), (to_partner.at[1, n], from_partner.at[1, n]))[kind]
        return pltpu.make_async_remote_copy(
            src_ref=here,
            dst_ref=there,
            send_sem=part_send.at[kind, n],
            recv_sem=part_recv.at[kind, n],
            device_id=(pair_z, t) if kind == 1 else (z, partner),
            device_id_type=MESH,
        )

    def down(m, n):
        columns = pl.ds(pl.multiple_of(n * TILE, TILE), TILE)
        return dot(activated[m], weights[2, :, columns])

    def add_up(n):
        part_copy(0, n).wait_recv()
        to_pair[n] = (kept[n] + from_partner[0, n].astype(jnp.float32)).astype(jnp.bfloat16)
        part_copy(1, n).start()

    hidden(1 - half)

    @pl.loop(0, TILES)
    def _(n):
        to_partner[0, n] = down(1 - core, n).astype(jnp.bfloat16)
        part_copy(0, n).start()
        kept[n] = down(core, n)

        @pl.when(n > 0)
        def _():
            add_up(n - 1)

    add_up(TILES - 1)

    hidden(half)

    @pl.loop(0, TILES)
    def _(n):
        to_partner[1, n] = down(1 - core, n).astype(jnp.bfloat16)
        part_copy(2, n).start()
        own_sum[n] = down(core, n)

    for n in range(TILES):
        part_copy(2, n).wait_recv()
        part_copy(1, n).wait_recv()
        columns = slice(n * TILE, (n + 1) * TILE)
        for j in range(2):
            rows = slice(j * NEW, (j + 1) * NEW)
            row = lax.broadcasted_iota(jnp.int32, (NEW, TILE), 0)
            total = (
                residual[j, :, columns].astype(jnp.float32)
                + own_sum[n, rows]
                + from_partner[1, n, rows].astype(jnp.float32)
                + from_pair[n, rows].astype(jnp.float32)
            )
            tokens[j, :, columns] = jnp.where(row < index_ref[64 + j], total, 0.0).astype(jnp.bfloat16)
    store = pltpu.make_async_copy(tokens, layer_hbm, local_sem.at[1])
    store.start()

    for part in range(2):
        for step in range(1, 4):
            source = lax.rem(z - step + 4, 4)
            pltpu.make_async_remote_copy(
                src_ref=arranged.at[part, pl.ds(0, 16)],
                dst_ref=arrived_hbm.at[part, source],
                send_sem=deal_send.at[part, step],
                recv_sem=deal_recv.at[part, step],
                device_id=(source, t),
                device_id_type=MESH,
            ).wait_recv()
            deal_copy(part, step).wait_send()
        own_deal(part).wait()

        @pl.loop(1, 32)
        def _(step):
            kv_copy(part, step).wait_send()

    for kind in range(3):
        for j in range(2):
            post_copy(kind, j).wait_send()
        for n in range(TILES):
            part_copy(kind, n).wait_send()
    store.wait()


def gather_kernel(index_ref, arrived_hbm, out_hbm, rows, load_sem, store_sem):
    def load(s, part):
        source = index_ref[s]
        return pltpu.make_async_copy(
            arrived_hbm.at[part, source // 16, lax.rem(source, 16)],
            rows.at[s, :, pl.ds(part * KEYS, KEYS)],
            load_sem.at[s // 16],
        )

    def store(block):
        span = pl.ds(pl.multiple_of(block * 16, 16), 16)
        return pltpu.make_async_copy(rows.at[span], out_hbm.at[span], store_sem.at[block])

    @pl.loop(0, 64)
    def _(s):
        load(s, 0).start()
        load(s, 1).start()

    @pl.loop(0, 4)
    def _(block):
        span = pl.ds(pl.multiple_of(block * 16, 16), 16)
        pltpu.make_async_copy(rows.at[span], rows.at[span], load_sem.at[block]).wait()
        store(block).start()

    @pl.loop(0, 4)
    def _(block):
        store(block).wait()


def lookup(source_table, wanted):
    every_index = jnp.arange(source_table.shape[0], dtype=jnp.int32)
    matches = wanted[:, None] == every_index[None, :]
    return jnp.sum(jnp.where(matches, source_table[None, :], 0), axis=1)


def locate(source_table, wanted):
    every_index = jnp.arange(source_table.shape[0], dtype=jnp.int32)
    matches = source_table[None, :] == wanted[:, None]
    return jnp.sum(jnp.where(matches, every_index[None, :], 0), axis=1)


def frequencies():
    lane = np.arange(LANES) % HEAD_DIM
    return rope_base ** (-2.0 * (lane % (HEAD_DIM // 2)) / HEAD_DIM), np.where(lane < HEAD_DIM // 2, -1.0, 1.0)


def local(
    tokens,
    cached,
    norm_gains,
    w_qkv,
    w_out,
    mlp_weights,
    request_order,
    new_lengths,
    cached_lengths,
    decode_slots,
):
    group_reqs = 64
    local_reqs = 2
    group_index = lax.axis_index("dp")
    device_index = group_index * 32 + lax.axis_index("tensor")
    local_order = lax.dynamic_slice_in_dim(request_order, device_index * local_reqs, local_reqs)
    new_counts = lookup(new_lengths, local_order)
    cached_counts = lookup(cached_lengths, local_order)

    group_order = lax.dynamic_slice_in_dim(request_order, group_index * group_reqs, group_reqs)
    row_slots = lookup(decode_slots, group_order)
    ordinal = jnp.arange(group_reqs, dtype=jnp.int32)
    rank = jnp.sum((row_slots[None, :] < row_slots[:, None]).astype(jnp.int32), axis=1)
    by_slot = jnp.sum(jnp.where(rank[None, :] == ordinal[:, None], ordinal[None, :], 0), axis=1)
    slot_ids = group_index * group_reqs + ordinal
    owners = locate(request_order, locate(decode_slots, slot_ids)) // group_reqs
    same_owner = (owners[:, None] == owners[None, :]) & (ordinal[None, :] < ordinal[:, None])
    source_rows = owners * 16 + jnp.sum(same_owner.astype(jnp.int32), axis=1)

    frequency, sign = frequencies()
    angle = np.arange(NEW)[:, None] * frequency[None, :]
    rope = jnp.asarray(np.stack([np.cos(angle), np.sin(angle)]), jnp.float32)
    turn = cached_counts.astype(jnp.float32)[:, None] * jnp.asarray(frequency, jnp.float32)[None, :]
    cosine, sine = jnp.cos(turn), jnp.sin(turn)
    signs = jnp.asarray(sign, jnp.float32)[None, :]
    turns = jnp.stack([cosine, sine, sine * signs, cosine * signs], axis=1)

    index = jnp.concatenate([by_slot, new_counts, cached_counts])
    own = jnp.transpose(mlp_weights, (0, 2, 1))

    bf16 = jnp.bfloat16
    smem = pl.BlockSpec(memory_space=pltpu.SMEM)
    vmem = pl.BlockSpec(memory_space=pltpu.VMEM)
    anywhere = pl.BlockSpec(memory_space=pl.ANY)
    dma = pltpu.SemaphoreType.DMA
    layer_out, arrived = pl.pallas_call(
        layer_kernel,
        out_shape=(
            jax.ShapeDtypeStruct((2, NEW, D), bf16),
            jax.ShapeDtypeStruct((2, 4, 16, 16, KEYS), bf16),
        ),
        in_specs=[smem, anywhere, anywhere, vmem, vmem, vmem, anywhere, anywhere, anywhere],
        out_specs=(anywhere, anywhere),
        scratch_shapes=[
            pltpu.VMEM((2, NEW, D), bf16),
            pltpu.VMEM((2 * NEW, D), bf16),
            pltpu.VMEM((D, 2 * D), bf16),
            pltpu.VMEM((D, D), bf16),
            pltpu.VMEM((2, CTX, D), bf16),
            pltpu.VMEM((3, 1024, D), bf16),
            pltpu.VMEM((2, NEW, D), bf16),
            pltpu.VMEM((2, NEW, D), bf16),
            pltpu.VMEM((2, NEW, D), bf16),
            pltpu.VMEM((2, NEW, D), bf16),
            pltpu.VMEM((4, 2 * NEW, D), bf16),
            pltpu.VMEM((32, 2, 16, KEYS), bf16),
            pltpu.VMEM((32, 2, 16, KEYS), bf16),
            pltpu.VMEM((2, 64, 16, KEYS), bf16),
            pltpu.VMEM((2, 2 * NEW, 1024), bf16),
            pltpu.VMEM((TILES, 2 * NEW, TILE), jnp.float32),
            pltpu.VMEM((TILES, 2 * NEW, TILE), jnp.float32),
            pltpu.VMEM((2, TILES, 2 * NEW, TILE), bf16),
            pltpu.VMEM((2, TILES, 2 * NEW, TILE), bf16),
            pltpu.VMEM((TILES, 2 * NEW, TILE), bf16),
            pltpu.VMEM((TILES, 2 * NEW, TILE), bf16),
            dma((5,)),
            dma((N_MSG,)),
            dma((N_MSG,)),
            dma((2, 32)),
            dma((2, 32)),
            dma((2, 4)),
            dma((2, 4)),
            dma((3, 2)),
            dma((3, 2)),
            dma((3, TILES)),
            dma((3, TILES)),
        ],
        compiler_params=pltpu.CompilerParams(
            collective_id=0, has_side_effects=True, vmem_limit_bytes=67_000_000
        ),
        name="layer",
    )(index, tokens, cached, norm_gains, turns, rope, w_qkv, w_out, own)

    kv_decode = pl.pallas_call(
        gather_kernel,
        out_shape=jax.ShapeDtypeStruct((64, 16, D), bf16),
        in_specs=[smem, anywhere],
        out_specs=anywhere,
        scratch_shapes=[pltpu.VMEM((64, 16, D), bf16), dma((4,)), dma((4,))],
        name="gather",
    )(source_rows, arrived)
    return (layer_out, kv_decode)


def solution(mesh):
    in_specs = (
        P(("dp", "tensor"), None, None),
        P(("dp", "tensor"), None, None),
        P(),
        P(),
        P(),
        P(None, None, "tensor"),
        P(),
        P(),
        P(),
        P(),
    )
    out_specs = (P(("dp", "tensor"), None, None), P("dp", "tensor", None))
    return jax.shard_map(local, mesh=mesh, in_specs=in_specs, out_specs=out_specs, check_vma=False)
```

time: 250 us -> 173 us (0.69); the launches traced: 245 us -> 172 us
  Pallas kernels: 0 us -> 161 us
  local copies, waits for them, and re-layouts: 66.9 us -> 4.77 us
  matrix products: 51.7 us -> 0 us
  waiting for transfers between devices: 47.8 us -> 0 us
  other arithmetic: 50.5 us -> 5.79 us
  between operations: 14.4 us -> 0.7 us
  starting transfers between devices: 13.3 us -> 0 us
    pallas_call x0 -> x2, Pallas kernels: none -> 161 us  [the longest x1 156 us: local(): pl.pallas_call(layer_kernel, out_shape=(jax.ShapeDtypeStruct((2, NEW, D),...]
    all_to_all x2 -> x0, waiting for transfers between devices: 47.8 us -> none  [the longest x1 47.8 us: local(): lax.all_to_all(contexts, 'tensor', split_axis=1, concat_axis=0, tiled=True)]
    dot_general x7 -> x0, matrix products: 41.5 us -> none  [the longest x1 11.5 us: block_sums(): jnp.einsum('rmw,dmw->mrd', spread, down_spread, preferred_element_type=jn...]
    select_n x6 -> x1, other arithmetic: 23.9 us -> 0.01 us  [local(): owners = locate(request_order, locate(decode_slots, slot_ids)) // group_reqs]
    slice x9 -> x0, local copies, waits for them, and re-layouts: 17.7 us -> none  [the longest x1 10.5 us: local(): mlp_sum = block_sums(activated, shards[2], unit_width)]
    all_to_all x2 -> x0, starting transfers between devices: 13.3 us -> none  [the longest x1 7.97 us: local(): lax.all_to_all(contexts, 'tensor', split_axis=1, concat_axis=0, tiled=True)]
    scatter x5 -> x0, other arithmetic: 12 us -> none
    sub x2 -> x0, matrix products: 10.2 us -> none  [attend(): exponent = jnp.exp(scores - highest)]
  transfers between devices with their start and end apart: 3 -> 0, of which waited for: 1 -> 0; matrix products, arithmetic and copies ran while one was open for 52% -> 0% of each run, Pallas kernels for 0% -> 0%
where the time goes in v1:
time: 173 us; the launch traced here: 172 us
  Pallas kernels  161 us (93%)
  other arithmetic  5.79 us (3%)
  local copies, waits for them, and re-layouts  4.77 us (3%)
    pallas_call x1, Pallas kernels, local(): pl.pallas_call(layer_kernel, out_shape=(jax.ShapeDtypeStruct((2, NEW, D),...  156 us
    pallas_call x1, Pallas kernels, local(): pl.pallas_call(gather_kernel, out_shape=jax.ShapeDtypeStruct((64, 16, D),...  4.54 us

profile of v1, /device:TPU:66, one launch (start us, length us, event | category | flops | bytes accessed | tf_op | source)
XLA Modules:
  0.0 172.3 jit_solution(473690380085741040)
XLA Ops:
  0.6 0.8 dynamic_slice.6
  1.4 0.8 dynamic_slice.7
  2.1 0.9 select_reduce_fusion.1
  3.0 0.9 select_reduce_fusion
  3.9 0.2 convert_reduce_fusion
  4.1 0.6 multiply_add_fusion.index_ref
  4.6 0.2 convert_reduce_fusion.1
  4.8 0.1 select_reduce_fusion.3
  4.9 0.9 select_reduce_fusion.5
  5.8 0.6 pad_add_fusion.index_ref
  6.5 0.9 broadcast_multiply_fusion.1
  7.4 0.6 pad_maximum_fusion.turn_ref
  8.0 2.4 %copy.18 = bf16[3,1536,128]{1,2,0:T(8,128)(2,1)} copy(bf16[3,1536,128]{2,1,0:T(8,128)(2,1)} %param.18) | data formatting | bytes 2359296 | tf_op args[5]
  10.3 156.5 %layer.1 = (bf16[2,128,1536]{2,1,0:T(8,128)(2,1)}, bf16[2,4,16,16,768]{4,3,2,1,0:T(8,128)(2,1)}) custom-call(s32[68]{0:T(128)} %pad_add_fusion.index_ref, bf16[2,128,1536]{2,1,0:T(8,128)(2,1)} %tokens_hbm.1, bf16[2,512,1536]{2,1,0:T(8,128)(2,1)} %cached_hbm.1, f32[2,1536]{1,0:T(2,128)} %gains_ref.1, f32[2,4,384]{2,1,0:T(4,128)} %pad_maximum_fusion.turn_ref, ...), custom_call_target="tpu_custom_call" | custom-call | tf_op jit(solution)/shard_map/layer/pallas_call | solution.py:616
  166.8 0.0 copy-start
  166.8 4.5 %gather.1 = bf16[64,16,1536]{2,1,0:T(8,128)(2,1)} custom-call(s32[64]{0:T(128)} %multiply_add_fusion.index_ref, bf16[2,4,16,16,768]{4,3,2,1,0:T(8,128)(2,1)} %get-tuple-element.5.arrived_hbm), custom_call_target="tpu_custom_call" | custom-call | tf_op jit(solution)/shard_map/gather/pallas_call | solution.py:664
  171.4 0.0 copy-done
  171.4 0.9 copy.20
  (3 shorter events, 0.0 us)
Async XLA Ops:
  166.8 4.6 %copy-start = (bf16[2,128,1536]{2,1,0:T(8,128)(2,1)S(1)}, bf16[2,128,1536]{2,1,0:T(8,128)(2,1)}, u32[]{:S(2)}) copy-start(bf16[2,128,1536]{2,1,0:T(8,128)(2,1)} %get-tuple-element.16) | copy-start | bytes 2359300

commit v2 on v1

--- a/solution.py
+++ b/solution.py
@@ -24,6 +24,8 @@
 LANES = 384
 TILE = 256
 TILES = D // TILE
+PARTS = 4
+WIDE = D // PARTS
 
 
 def messages():
@@ -96,17 +98,22 @@
 
 
 def layer_kernel(
-    index_ref,
+    order_ref,
+    new_ref,
+    prefix_ref,
+    slots_ref,
     tokens_hbm,
     cached_hbm,
     gains_ref,
-    turn_ref,
     rope_ref,
     w_qkv_hbm,
     w_out_hbm,
     own_hbm,
     layer_hbm,
     arrived_hbm,
+    source_ref,
+    by_slot,
+    by_slot_rows,
     tokens,
     normed,
     w_qkv,
@@ -118,8 +125,10 @@
     attended,
     residual,
     posts,
-    received_keys,
-    received_values,
+    received_0,
+    received_1,
+    received_2,
+    received_3,
     arranged,
     activated,
     kept,
@@ -148,6 +157,10 @@
     partner = t + 1 - 2 * core
     member = half * 2 + core
 
+    requests = [order_ref[(z * 32 + t) * 2 + j] for j in range(2)]
+    new_counts = [new_ref[request] for request in requests]
+    cached_counts = [prefix_ref[request] for request in requests]
+
     def tensor_at(dx, dy, other=0):
         there = lax.rem(core + other, 2)
         return (lax.rem(x + dx + RING, RING) * RING + lax.rem(y + dy + RING, RING)) * 2 + there
@@ -220,12 +233,11 @@
                         weight_arrival(other)
                 weight_copy(index).start()
 
-    def weight_rest():
+    def weight_ready(column):
         for index in range(N_MSG):
-            if index not in heard:
+            if index not in heard and arrival(MESSAGES[index])[0][0] == column:
+                heard.add(index)
                 weight_arrival(index)
-        for index in range(N_MSG):
-            weight_copy(index).wait_send()
 
     loads[0].wait()
     weight_stage(0)
@@ -239,8 +251,11 @@
     leading = lax.rem(lane, HEAD_DIM) < HEAD_DIM // 2
 
     def rotated(values, j):
-        cosine = turn_ref[j, 0:1, :] * rope_ref[0] - turn_ref[j, 1:2, :] * rope_ref[1]
-        sine = turn_ref[j, 2:3, :] * rope_ref[0] + turn_ref[j, 3:4, :] * rope_ref[1]
+        turn = cached_counts[j].astype(jnp.float32) * rope_ref[2, 0:8, :]
+        turn_cosine, turn_sine = jnp.cos(turn)[0:1], jnp.sin(turn)[0:1]
+        cosine = turn_cosine * rope_ref[0] - turn_sine * rope_ref[1]
+        sine = turn_sine * rope_ref[0] + turn_cosine * rope_ref[1]
+        sine = jnp.where(leading, -sine, sine)
         parts = []
         for n in range(values.shape[1] // LANES):
             part = values[:, n * LANES : (n + 1) * LANES]
@@ -267,7 +282,8 @@
     @pl.loop(0, 8)
     def _(step):
         j, block = step // 4, lax.rem(step, 4)
-        new_count, cached_count = index_ref[64 + j], index_ref[66 + j]
+        new_count = new_ref[order_ref[(z * 32 + t) * 2 + j]]
+        cached_count = prefix_ref[order_ref[(z * 32 + t) * 2 + j]]
         spot = block * 128 + lax.broadcasted_iota(jnp.int32, (128, NEW), 0)
         order = lax.broadcasted_iota(jnp.int32, (128, NEW), 1)
         chosen = (spot - cached_count == order) & (order < new_count)
@@ -276,12 +292,15 @@
         row = block * 128 + lax.broadcasted_iota(jnp.int32, (128, D), 0)
         context[j, rows, :] = jnp.where(row < cached_count, context[j, rows, :], placed)
 
-    received = (received_keys, received_values)
+    received = (received_0, received_1, received_2, received_3)
+
+    def offset_at(step):
+        turn, dx = step // 8, lax.rem(step // 2, RING)
+        return dx, lax.rem(turn + dx, RING), lax.rem(step, 2)
 
     def kv_copy(part, step):
-        dx, dy, dc = step // 8, lax.rem(step // 2, RING), lax.rem(step, 2)
-        target = tensor_at(dx, dy, dc)
-        columns = pl.ds(part * KEYS, KEYS)
+        target = tensor_at(*offset_at(step))
+        columns = pl.ds(part * WIDE, WIDE)
         return pltpu.make_async_remote_copy(
             src_ref=context.at[:, pl.ds(pl.multiple_of(target * 16, 16), 16), columns],
             dst_ref=received[part].at[t],
@@ -291,17 +310,18 @@
             device_id_type=MESH,
         )
 
-    for part in range(2):
-
+    def kv_start(part):
         @pl.loop(1, 32)
         def _(step):
             kv_copy(part, step).start()
 
-    for part in range(2):
         for j in range(2):
             received[part][t, j] = context[
-                j, pl.ds(pl.multiple_of(t * 16, 16), 16), part * KEYS : (part + 1) * KEYS
+                j, pl.ds(pl.multiple_of(t * 16, 16), 16), part * WIDE : (part + 1) * WIDE
             ]
+
+    for part in range(PARTS):
+        kv_start(part)
 
     for n in range(2):
         some = project(n * KEYS)
@@ -310,8 +330,36 @@
 
     weight_stage(1)
 
+    along = lax.broadcasted_iota(jnp.int32, (64, 128), 1)
+    across = lax.broadcasted_iota(jnp.int32, (64, 128), 0)
+    spread = lax.broadcasted_iota(jnp.int32, (1, 128), 1)
+    inside = along < 64
+
+    def upright(row):
+        return jnp.sum(jnp.where(along == across, row, 0), axis=1, keepdims=True)
+
+    def add_slot(i, row):
+        return jnp.where(spread == i, slots_ref[order_ref[z * 64 + i]], row)
+
+    slots = lax.fori_loop(0, 64, add_slot, jnp.zeros((1, 128), jnp.int32))
+    rank = jnp.sum(
+        jnp.where((slots < upright(slots)) & inside, 1, 0), axis=1, keepdims=True
+    )
+    by_slot[...] = jnp.sum(jnp.where(rank == along, across, 0), axis=0, keepdims=True)
+
+    def add_owner(i, row):
+        return jnp.where(spread == slots_ref[order_ref[i]] - z * 64, i // 64, row)
+
+    owners = lax.fori_loop(0, 256, add_owner, jnp.zeros((1, 128), jnp.int32))
+    owner = upright(owners)
+    earlier = jnp.sum(
+        jnp.where((owner == owners) & (along < across), 1, 0), axis=1, keepdims=True
+    )
+    source = jnp.minimum(owner * 16 + earlier, 63)
+    source_ref[...] = jnp.sum(jnp.where(along == across, source, 0), axis=0, keepdims=True)
+
     def attend(j):
-        cached_count = index_ref[66 + j]
+        cached_count = cached_counts[j]
         spot = lax.broadcasted_iota(jnp.int32, (2 * NEW, CTX), 1)
         order = lax.rem(lax.broadcasted_iota(jnp.int32, (2 * NEW, CTX), 0), NEW)
         allowed = spot <= cached_count + order
@@ -366,10 +414,6 @@
         posts[member, pl.ds(j * NEW, NEW), :] = norm_rows(rounded, gains_ref[1:2, :])
         post_copy(1, j).start()
         post_copy(0, j).start()
-        if j == 0:
-            weight_stage(2)
-
-    weight_stage(3)
 
     def deal_copy(part, step):
         target = lax.rem(z + step, 4)
@@ -392,7 +436,7 @@
     def deal(part):
         @pl.loop(1, 32)
         def _(step):
-            dx, dy, dc = step // 8, lax.rem(step // 2, RING), lax.rem(step, 2)
+            dx, dy, dc = offset_at(step)
             source = (
                 lax.rem(x - dx + RING, RING) * RING + lax.rem(y - dy + RING, RING)
             ) * 2 + lax.rem(core + dc, 2)
@@ -407,34 +451,49 @@
 
         @pl.loop(0, 64)
         def _(row):
-            slot = index_ref[row]
+            slot = lax.rem(by_slot_rows[0, row], 64)
             arranged[part, row] = received[part][slot // 2, lax.rem(slot, 2)]
 
         for step in range(1, 4):
             deal_copy(part, step).start()
         own_deal(part).start()
 
-    for j in range(2):
-        post_arrival(1, j)
-        post_copy(2, j).start()
-
+    ordering = pltpu.make_async_copy(by_slot, by_slot_rows, local_sem.at[0])
+    ordering.start()
+    ordering.wait()
     deal(0)
     deal(1)
+    post_arrival(1, 0)
+    post_copy(2, 0).start()
+    deal(2)
+    post_arrival(1, 1)
+    post_copy(2, 1).start()
+    deal(3)
+
+    def hidden(which, column):
+        units = pl.ds(pl.multiple_of(lax.rem(x + column, RING) * TILE, TILE), TILE)
+
+        @pl.loop(which * 2, which * 2 + 2)
+        def _(m):
+            rows = posts[m]
+            gate = dot_nt(rows, weights[0, units, :])
+            up = dot_nt(rows, weights[1, units, :])
+            activated[m, :, units] = (gate / (1.0 + jnp.exp(-gate)) * up).astype(jnp.bfloat16)
 
     for j in range(2):
         post_arrival(0, j)
         post_arrival(2, j)
-    weight_rest()
-
-    def hidden(which):
-        @pl.loop(0, 4)
-        def _(step):
-            units = pl.ds(pl.multiple_of(step * TILE, TILE), TILE)
-            for m in range(2):
-                rows = posts[which * 2 + m]
-                gate = dot_nt(rows, weights[0, units, :])
-                up = dot_nt(rows, weights[1, units, :])
-                activated[m, :, units] = (gate / (1.0 + jnp.exp(-gate)) * up).astype(jnp.bfloat16)
+    weight_stage(2)
+    weight_ready(0)
+    hidden(1 - half, 0)
+    hidden(half, 0)
+    weight_stage(3)
+    weight_ready(1)
+    hidden(1 - half, 1)
+    weight_ready(3)
+    hidden(1 - half, 3)
+    weight_ready(2)
+    hidden(1 - half, 2)
 
     def part_copy(kind, n):
         here, there = ((to_partner.at[0, n], from_partner.at[0, n]), (to_pair.at[n], from_pair.at[n]), (to_partner.at[1, n], from_partner.at[1, n]))[kind]
@@ -447,22 +506,20 @@
             device_id_type=MESH,
         )
 
-    def down(m, n):
+    def down(which, core_at, n):
         columns = pl.ds(pl.multiple_of(n * TILE, TILE), TILE)
-        return dot(activated[m], weights[2, :, columns])
+        return dot(activated[which * 2 + core_at], weights[2, :, columns])
 
     def add_up(n):
         part_copy(0, n).wait_recv()
         to_pair[n] = (kept[n] + from_partner[0, n].astype(jnp.float32)).astype(jnp.bfloat16)
         part_copy(1, n).start()
 
-    hidden(1 - half)
-
     @pl.loop(0, TILES)
     def _(n):
-        to_partner[0, n] = down(1 - core, n).astype(jnp.bfloat16)
+        to_partner[0, n] = down(1 - half, 1 - core, n).astype(jnp.bfloat16)
         part_copy(0, n).start()
-        kept[n] = down(core, n)
+        kept[n] = down(1 - half, core, n)
 
         @pl.when(n > 0)
         def _():
@@ -470,13 +527,14 @@
 
     add_up(TILES - 1)
 
-    hidden(half)
+    for column in (1, 3, 2):
+        hidden(half, column)
 
     @pl.loop(0, TILES)
     def _(n):
-        to_partner[1, n] = down(1 - core, n).astype(jnp.bfloat16)
+        to_partner[1, n] = down(half, 1 - core, n).astype(jnp.bfloat16)
         part_copy(2, n).start()
-        own_sum[n] = down(core, n)
+        own_sum[n] = down(half, core, n)
 
     for n in range(TILES):
         part_copy(2, n).wait_recv()
@@ -491,11 +549,11 @@
                 + from_partner[1, n, rows].astype(jnp.float32)
                 + from_pair[n, rows].astype(jnp.float32)
             )
-            tokens[j, :, columns] = jnp.where(row < index_ref[64 + j], total, 0.0).astype(jnp.bfloat16)
+            tokens[j, :, columns] = jnp.where(row < new_counts[j], total, 0.0).astype(jnp.bfloat16)
     store = pltpu.make_async_copy(tokens, layer_hbm, local_sem.at[1])
     store.start()
 
-    for part in range(2):
+    for part in range(PARTS):
         for step in range(1, 4):
             source = lax.rem(z - step + 4, 4)
             pltpu.make_async_remote_copy(
@@ -513,6 +571,8 @@
         def _(step):
             kv_copy(part, step).wait_send()
 
+    for index in range(N_MSG):
+        weight_copy(index).wait_send()
     for kind in range(3):
         for j in range(2):
             post_copy(kind, j).wait_send()
@@ -523,10 +583,10 @@
 
 def gather_kernel(index_ref, arrived_hbm, out_hbm, rows, load_sem, store_sem):
     def load(s, part):
-        source = index_ref[s]
+        source = index_ref[0, s]
         return pltpu.make_async_copy(
             arrived_hbm.at[part, source // 16, lax.rem(source, 16)],
-            rows.at[s, :, pl.ds(part * KEYS, KEYS)],
+            rows.at[s, :, pl.ds(part * WIDE, WIDE)],
             load_sem.at[s // 16],
         )
 
@@ -536,8 +596,8 @@
 
     @pl.loop(0, 64)
     def _(s):
-        load(s, 0).start()
-        load(s, 1).start()
+        for part in range(PARTS):
+            load(s, part).start()
 
     @pl.loop(0, 4)
     def _(block):
@@ -550,21 +610,9 @@
         store(block).wait()
 
 
-def lookup(source_table, wanted):
-    every_index = jnp.arange(source_table.shape[0], dtype=jnp.int32)
-    matches = wanted[:, None] == every_index[None, :]
-    return jnp.sum(jnp.where(matches, source_table[None, :], 0), axis=1)
-
-
-def locate(source_table, wanted):
-    every_index = jnp.arange(source_table.shape[0], dtype=jnp.int32)
-    matches = source_table[None, :] == wanted[:, None]
-    return jnp.sum(jnp.where(matches, every_index[None, :], 0), axis=1)
-
-
 def frequencies():
     lane = np.arange(LANES) % HEAD_DIM
-    return rope_base ** (-2.0 * (lane % (HEAD_DIM // 2)) / HEAD_DIM), np.where(lane < HEAD_DIM // 2, -1.0, 1.0)
+    return rope_base ** (-2.0 * (lane % (HEAD_DIM // 2)) / HEAD_DIM)
 
 
 def local(
@@ -579,33 +627,10 @@
     cached_lengths,
     decode_slots,
 ):
-    group_reqs = 64
-    local_reqs = 2
-    group_index = lax.axis_index("dp")
-    device_index = group_index * 32 + lax.axis_index("tensor")
-    local_order = lax.dynamic_slice_in_dim(request_order, device_index * local_reqs, local_reqs)
-    new_counts = lookup(new_lengths, local_order)
-    cached_counts = lookup(cached_lengths, local_order)
-
-    group_order = lax.dynamic_slice_in_dim(request_order, group_index * group_reqs, group_reqs)
-    row_slots = lookup(decode_slots, group_order)
-    ordinal = jnp.arange(group_reqs, dtype=jnp.int32)
-    rank = jnp.sum((row_slots[None, :] < row_slots[:, None]).astype(jnp.int32), axis=1)
-    by_slot = jnp.sum(jnp.where(rank[None, :] == ordinal[:, None], ordinal[None, :], 0), axis=1)
-    slot_ids = group_index * group_reqs + ordinal
-    owners = locate(request_order, locate(decode_slots, slot_ids)) // group_reqs
-    same_owner = (owners[:, None] == owners[None, :]) & (ordinal[None, :] < ordinal[:, None])
-    source_rows = owners * 16 + jnp.sum(same_owner.astype(jnp.int32), axis=1)
-
-    frequency, sign = frequencies()
+    frequency = frequencies()
     angle = np.arange(NEW)[:, None] * frequency[None, :]
-    rope = jnp.asarray(np.stack([np.cos(angle), np.sin(angle)]), jnp.float32)
-    turn = cached_counts.astype(jnp.float32)[:, None] * jnp.asarray(frequency, jnp.float32)[None, :]
-    cosine, sine = jnp.cos(turn), jnp.sin(turn)
-    signs = jnp.asarray(sign, jnp.float32)[None, :]
-    turns = jnp.stack([cosine, sine, sine * signs, cosine * signs], axis=1)
-
-    index = jnp.concatenate([by_slot, new_counts, cached_counts])
+    tables = [np.cos(angle), np.sin(angle), np.broadcast_to(frequency, angle.shape)]
+    rope = jnp.asarray(np.stack(tables), jnp.float32)
     own = jnp.transpose(mlp_weights, (0, 2, 1))
 
     bf16 = jnp.bfloat16
@@ -613,15 +638,18 @@
     vmem = pl.BlockSpec(memory_space=pltpu.VMEM)
     anywhere = pl.BlockSpec(memory_space=pl.ANY)
     dma = pltpu.SemaphoreType.DMA
-    layer_out, arrived = pl.pallas_call(
+    layer_out, arrived, source_rows = pl.pallas_call(
         layer_kernel,
         out_shape=(
             jax.ShapeDtypeStruct((2, NEW, D), bf16),
-            jax.ShapeDtypeStruct((2, 4, 16, 16, KEYS), bf16),
+            jax.ShapeDtypeStruct((PARTS, 4, 16, 16, WIDE), bf16),
+            jax.ShapeDtypeStruct((1, 128), jnp.int32),
         ),
-        in_specs=[smem, anywhere, anywhere, vmem, vmem, vmem, anywhere, anywhere, anywhere],
-        out_specs=(anywhere, anywhere),
+        in_specs=[smem] * 4 + [anywhere, anywhere, vmem, vmem, anywhere, anywhere, anywhere],
+        out_specs=(anywhere, anywhere, vmem),
         scratch_shapes=[
+            pltpu.VMEM((1, 128), jnp.int32),
+            pltpu.SMEM((1, 128), jnp.int32),
             pltpu.VMEM((2, NEW, D), bf16),
             pltpu.VMEM((2 * NEW, D), bf16),
             pltpu.VMEM((D, 2 * D), bf16),
@@ -633,10 +661,9 @@
             pltpu.VMEM((2, NEW, D), bf16),
             pltpu.VMEM((2, NEW, D), bf16),
             pltpu.VMEM((4, 2 * NEW, D), bf16),
-            pltpu.VMEM((32, 2, 16, KEYS), bf16),
-            pltpu.VMEM((32, 2, 16, KEYS), bf16),
-            pltpu.VMEM((2, 64, 16, KEYS), bf16),
-            pltpu.VMEM((2, 2 * NEW, 1024), bf16),
+            *[pltpu.VMEM((32, 2, 16, WIDE), bf16) for _ in range(PARTS)],
+            pltpu.VMEM((PARTS, 64, 16, WIDE), bf16),
+            pltpu.VMEM((4, 2 * NEW, 1024), bf16),
             pltpu.VMEM((TILES, 2 * NEW, TILE), jnp.float32),
             pltpu.VMEM((TILES, 2 * NEW, TILE), jnp.float32),
             pltpu.VMEM((2, TILES, 2 * NEW, TILE), bf16),
@@ -646,10 +673,10 @@
             dma((5,)),
             dma((N_MSG,)),
             dma((N_MSG,)),
-            dma((2, 32)),
-            dma((2, 32)),
-            dma((2, 4)),
-            dma((2, 4)),
+            dma((PARTS, 32)),
+            dma((PARTS, 32)),
+            dma((PARTS, 4)),
+            dma((PARTS, 4)),
             dma((3, 2)),
             dma((3, 2)),
             dma((3, TILES)),
@@ -659,7 +686,19 @@
             collective_id=0, has_side_effects=True, vmem_limit_bytes=67_000_000
         ),
         name="layer",
-    )(index, tokens, cached, norm_gains, turns, rope, w_qkv, w_out, own)
+    )(
+        request_order,
+        new_lengths,
+        cached_lengths,
+        decode_slots,
+        tokens,
+        cached,
+        norm_gains,
+        rope,
+        w_qkv,
+        w_out,
+        own,
+    )
 
     kv_decode = pl.pallas_call(
         gather_kernel,

time: 173 us -> 130 us (0.75)
  Pallas kernels: 161 us -> 125 us
  other arithmetic: 5.79 us -> 0 us
    pallas_call x1, Pallas kernels: 156 us -> 120 us  [local(): pl.pallas_call(layer_kernel, out_shape=(jax.ShapeDtypeStruct((2, NEW, D),...]
    reduce_sum x6 -> x0, other arithmetic: 3.11 us -> none  [the longest x2 1.72 us: locate(): return jnp.sum(jnp.where(matches, every_index[None, :], 0), axis=1)]
where the time goes in v2:
time: 130 us; the launch traced here: 129 us
  Pallas kernels  125 us (96%)
  local copies, waits for them, and re-layouts  3.27 us (3%)
    pallas_call x1, Pallas kernels, local(): pl.pallas_call(layer_kernel, out_shape=(jax.ShapeDtypeStruct((2, NEW, D),...  120 us
    pallas_call x1, Pallas kernels, local(): pl.pallas_call(gather_kernel, out_shape=jax.ShapeDtypeStruct((64, 16, D),...  5.15 us
    unnamed x4, local copies, waits for them, and re-layouts  3.27 us

profile of v2, /device:TPU:66, one launch (start us, length us, event | category | flops | bytes accessed | tf_op | source)
XLA Modules:
  0.0 129.2 jit_solution(12305881981607560477)
XLA Ops:
  0.6 2.4 %copy.13 = bf16[3,1536,128]{1,2,0:T(8,128)(2,1)} copy(bf16[3,1536,128]{2,1,0:T(8,128)(2,1)} %param.16) | data formatting | bytes 2359296 | tf_op args[5]
  3.0 120.1 %layer.1 = (bf16[2,128,1536]{2,1,0:T(8,128)(2,1)}, bf16[4,4,16,16,384]{4,3,2,1,0:T(8,128)(2,1)}, s32[1,128]{1,0:T(1,128)}) custom-call(s32[256]{0:T(256)} %order_ref.1, s32[256]{0:T(256)} %new_ref.1, s32[256]{0:T(256)} %prefix_ref.1, s32[256]{0:T(256)} %slots_ref.1, bf16[2,128,1536]{2,1,0:T(8,128)(2,1)} %tokens_hbm.1, bf16[2,512,1536]{2,1,0:T(8,128)(2,1)} %cached_hbm.1, ...), custom_call_target="tpu_custom_call" | custom-call | tf_op jit(solution)/shard_map/layer/pallas_call | solution.py:641
  123.1 0.0 copy-start
  123.1 5.2 %gather.1 = bf16[64,16,1536]{2,1,0:T(8,128)(2,1)} custom-call(s32[1,128]{1,0:T(1,128)} %get-tuple-element.6.index_ref, bf16[4,4,16,16,384]{4,3,2,1,0:T(8,128)(2,1)} %get-tuple-element.7.arrived_hbm), custom_call_target="tpu_custom_call" | custom-call | tf_op jit(solution)/shard_map/gather/pallas_call | solution.py:703
  128.3 0.0 copy-done
  128.3 0.9 copy.15
Async XLA Ops:
  123.1 5.2 %copy-start = (bf16[2,128,1536]{2,1,0:T(8,128)(2,1)S(1)}, bf16[2,128,1536]{2,1,0:T(8,128)(2,1)}, u32[]{:S(2)}) copy-start(bf16[2,128,1536]{2,1,0:T(8,128)(2,1)} %get-tuple-element.10) | copy-start | bytes 2359300

commit v3 on v2

--- a/solution.py
+++ b/solution.py
@@ -138,6 +138,7 @@
     to_pair,
     from_pair,
     local_sem,
+    store_sem,
     weight_send,
     weight_recv,
     kv_send,
@@ -224,9 +225,9 @@
 
     heard = set()
 
-    def weight_stage(number):
+    def weight_stage(number, kinds=("send", "pass")):
         for index in range(N_MSG):
-            if stage_of(index) == number:
+            if stage_of(index) == number and MESSAGES[index][4] in kinds:
                 for other in sources(index) if number else []:
                     if other not in heard:
                         heard.add(other)
@@ -320,8 +321,7 @@
                 j, pl.ds(pl.multiple_of(t * 16, 16), 16), part * WIDE : (part + 1) * WIDE
             ]
 
-    for part in range(PARTS):
-        kv_start(part)
+    kv_start(0)
 
     for n in range(2):
         some = project(n * KEYS)
@@ -329,6 +329,8 @@
             queries[j, :, n * KEYS : (n + 1) * KEYS] = rotated(some[j * NEW : (j + 1) * NEW], j)
 
     weight_stage(1)
+    for part in range(1, PARTS):
+        kv_start(part)
 
     along = lax.broadcasted_iota(jnp.int32, (64, 128), 1)
     across = lax.broadcasted_iota(jnp.int32, (64, 128), 0)
@@ -462,13 +464,13 @@
     ordering.start()
     ordering.wait()
     deal(0)
+    for j in range(2):
+        post_arrival(1, j)
+        post_copy(2, j).start()
+    weight_stage(2, ("send",))
+    weight_stage(2, ("pass",))
     deal(1)
-    post_arrival(1, 0)
-    post_copy(2, 0).start()
     deal(2)
-    post_arrival(1, 1)
-    post_copy(2, 1).start()
-    deal(3)
 
     def hidden(which, column):
         units = pl.ds(pl.multiple_of(lax.rem(x + column, RING) * TILE, TILE), TILE)
@@ -483,9 +485,9 @@
     for j in range(2):
         post_arrival(0, j)
         post_arrival(2, j)
-    weight_stage(2)
     weight_ready(0)
     hidden(1 - half, 0)
+    deal(3)
     hidden(half, 0)
     weight_stage(3)
     weight_ready(1)
@@ -535,6 +537,12 @@
         to_partner[1, n] = down(half, 1 - core, n).astype(jnp.bfloat16)
         part_copy(2, n).start()
         own_sum[n] = down(half, core, n)
+
+    def store(n):
+        columns = pl.ds(n * TILE, TILE)
+        return pltpu.make_async_copy(
+            tokens.at[:, :, columns], layer_hbm.at[:, :, columns], store_sem.at[n]
+        )
 
     for n in range(TILES):
         part_copy(2, n).wait_recv()
@@ -550,8 +558,7 @@
                 + from_pair[n, rows].astype(jnp.float32)
             )
             tokens[j, :, columns] = jnp.where(row < new_counts[j], total, 0.0).astype(jnp.bfloat16)
-    store = pltpu.make_async_copy(tokens, layer_hbm, local_sem.at[1])
-    store.start()
+        store(n).start()
 
     for part in range(PARTS):
         for step in range(1, 4):
@@ -578,36 +585,39 @@
             post_copy(kind, j).wait_send()
         for n in range(TILES):
             part_copy(kind, n).wait_send()
-    store.wait()
+    for n in range(TILES):
+        store(n).wait()
 
 
 def gather_kernel(index_ref, arrived_hbm, out_hbm, rows, load_sem, store_sem):
-    def load(s, part):
-        source = index_ref[0, s]
+    def span_at(block):
+        return pl.ds(pl.multiple_of(block * 16, 16), 16)
+
+    def store(block, part):
+        span = span_at(block)
         return pltpu.make_async_copy(
-            arrived_hbm.at[part, source // 16, lax.rem(source, 16)],
-            rows.at[s, :, pl.ds(part * WIDE, WIDE)],
-            load_sem.at[s // 16],
-        )
-
-    def store(block):
-        span = pl.ds(pl.multiple_of(block * 16, 16), 16)
-        return pltpu.make_async_copy(rows.at[span], out_hbm.at[span], store_sem.at[block])
+            rows.at[span, part],
+            out_hbm.at[span, :, pl.ds(part * WIDE, WIDE)],
+            store_sem.at[block, part],
+        )
 
     @pl.loop(0, 64)
     def _(s):
+        source = index_ref[0, s]
+        pltpu.make_async_copy(
+            arrived_hbm.at[:, source // 16, lax.rem(source, 16)],
+            rows.at[s],
+            load_sem.at[s // 16],
+        ).start()
+
+    for block in range(4):
+        span = span_at(block)
+        pltpu.make_async_copy(rows.at[span], rows.at[span], load_sem.at[block]).wait()
         for part in range(PARTS):
-            load(s, part).start()
-
-    @pl.loop(0, 4)
-    def _(block):
-        span = pl.ds(pl.multiple_of(block * 16, 16), 16)
-        pltpu.make_async_copy(rows.at[span], rows.at[span], load_sem.at[block]).wait()
-        store(block).start()
-
-    @pl.loop(0, 4)
-    def _(block):
-        store(block).wait()
+            store(block, part).start()
+    for block in range(4):
+        for part in range(PARTS):
+            store(block, part).wait()
 
 
 def frequencies():
@@ -671,6 +681,7 @@
             pltpu.VMEM((TILES, 2 * NEW, TILE), bf16),
             pltpu.VMEM((TILES, 2 * NEW, TILE), bf16),
             dma((5,)),
+            dma((TILES,)),
             dma((N_MSG,)),
             dma((N_MSG,)),
             dma((PARTS, 32)),
@@ -705,7 +716,7 @@
         out_shape=jax.ShapeDtypeStruct((64, 16, D), bf16),
         in_specs=[smem, anywhere],
         out_specs=anywhere,
-        scratch_shapes=[pltpu.VMEM((64, 16, D), bf16), dma((4,)), dma((4,))],
+        scratch_shapes=[pltpu.VMEM((64, PARTS, 16, WIDE), bf16), dma((4,)), dma((4, PARTS))],
         name="gather",
     )(source_rows, arrived)
     return (layer_out, kv_decode)

time: 130 us -> 127 us (0.977)
  Pallas kernels: 125 us -> 121 us
    pallas_call x1, Pallas kernels: 120 us -> 117 us  [local(): pl.pallas_call(layer_kernel, out_shape=(jax.ShapeDtypeStruct((2, NEW, D),...]
where the time goes in v3:
time: 127 us; the launch traced here: 125 us
  Pallas kernels  121 us (95%)
  local copies, waits for them, and re-layouts  3.27 us (3%)
    pallas_call x1, Pallas kernels, local(): pl.pallas_call(layer_kernel, out_shape=(jax.ShapeDtypeStruct((2, NEW, D),...  117 us
    pallas_call x1, Pallas kernels, local(): pl.pallas_call(gather_kernel, out_shape=jax.ShapeDtypeStruct((64, 16, D),...  3.9 us
    unnamed x4, local copies, waits for them, and re-layouts  3.27 us

profile of v3, /device:TPU:66, one launch (start us, length us, event | category | flops | bytes accessed | tf_op | source)
XLA Modules:
  0.0 125.2 jit_solution(16906507886389795292)
XLA Ops:
  0.6 2.4 %copy.13 = bf16[3,1536,128]{1,2,0:T(8,128)(2,1)} copy(bf16[3,1536,128]{2,1,0:T(8,128)(2,1)} %param.16) | data formatting | bytes 2359296 | tf_op args[5]
  3.0 117.3 %layer.1 = (bf16[2,128,1536]{2,1,0:T(8,128)(2,1)}, bf16[4,4,16,16,384]{4,3,2,1,0:T(8,128)(2,1)}, s32[1,128]{1,0:T(1,128)}) custom-call(s32[256]{0:T(256)} %order_ref.1, s32[256]{0:T(256)} %new_ref.1, s32[256]{0:T(256)} %prefix_ref.1, s32[256]{0:T(256)} %slots_ref.1, bf16[2,128,1536]{2,1,0:T(8,128)(2,1)} %tokens_hbm.1, bf16[2,512,1536]{2,1,0:T(8,128)(2,1)} %cached_hbm.1, ...), custom_call_target="tpu_custom_call" | custom-call | tf_op jit(solution)/shard_map/layer/pallas_call | solution.py:651
  120.4 0.0 copy-start
  120.4 3.9 %gather.1 = bf16[64,16,1536]{2,1,0:T(8,128)(2,1)} custom-call(s32[1,128]{1,0:T(1,128)} %get-tuple-element.6.index_ref, bf16[4,4,16,16,384]{4,3,2,1,0:T(8,128)(2,1)} %get-tuple-element.7.arrived_hbm), custom_call_target="tpu_custom_call" | custom-call | tf_op jit(solution)/shard_map/gather/pallas_call | solution.py:714
  124.3 0.0 copy-done
  124.3 0.9 copy.15
Async XLA Ops:
  120.4 3.9 %copy-start = (bf16[2,128,1536]{2,1,0:T(8,128)(2,1)S(1)}, bf16[2,128,1536]{2,1,0:T(8,128)(2,1)}, u32[]{:S(2)}) copy-start(bf16[2,128,1536]{2,1,0:T(8,128)(2,1)} %get-tuple-element.10) | copy-start | bytes 2359300
